TPU v7x, 32 devices: a whole 2x2x4 slice. The times are simulated.
32 devices in a mesh: dp: 8 (over y, x, core), tensor: 4 (over z).
Axes of the slice: x: 2, y: 2, z: 4, core: 2. Of those that a mesh axis runs over, the one named last changes fastest.
Arguments:
- inputs: bfloat16 [16, 1024, 1024], P('dp', 'tensor'), may hold values from -6 to 6
- lengths: int32 [16], P('dp'), may hold values from 256 to 1024, as said below
- w_query: bfloat16 [1024, 1024], P('dp', 'tensor'), may hold values from -0.1875 to 0.1875
- w_key: bfloat16 [1024, 1024], P('dp', 'tensor'), may hold values from -0.1875 to 0.1875
- w_value: bfloat16 [1024, 1024], P('dp', 'tensor'), may hold values from -0.1875 to 0.1875
- b_query: bfloat16 [1024], P('tensor'), may hold values from -3 to 3
- b_value: bfloat16 [1024], P('tensor'), may hold values from -0.29882812 to 0.29882812
- w_out: bfloat16 [1024, 1024], P('tensor', 'dp'), may hold values from -1.5 to 1.5
- b_out: bfloat16 [1024], replicated, may hold values from -3 to 3
- gain_one: bfloat16 [1024], replicated, may hold values from 0.099609375 to 1.8984375
- shift_one: bfloat16 [1024], replicated, may hold values from -3 to 3
- w_in: bfloat16 [1024, 4096], P('dp', 'tensor'), may hold values from -0.1875 to 0.1875
- b_in: bfloat16 [4096], P('tensor'), may hold values from -3 to 3
- w_back: bfloat16 [4096, 1024], P('tensor', 'dp'), may hold values from -0.09375 to 0.09375
- b_back: bfloat16 [1024], replicated, may hold values from -3 to 3
- gain_two: bfloat16 [1024], replicated, may hold values from 0.099609375 to 1.8984375
- shift_two: bfloat16 [1024], replicated, may hold values from -3 to 3
- cotangent: bfloat16 [16, 1024, 1024], P('dp', 'tensor'), may hold values from -6 to 6
Outputs:
- layer_out: bfloat16 [16, 1024, 1024], P('dp', 'tensor')
- grad_inputs: float32 [16, 1024, 1024], P('dp', 'tensor')
- grad_w_query: float32 [1024, 1024], P('dp', 'tensor')
- grad_w_key: float32 [1024, 1024], P('dp', 'tensor')
- grad_w_value: float32 [1024, 1024], P('dp', 'tensor')
- grad_b_query: float32 [1024], P('tensor')
- grad_b_value: float32 [1024], P('tensor')
- grad_w_out: float32 [1024, 1024], P('tensor', 'dp')
- grad_b_out: float32 [1024], replicated
- grad_gain_one: float32 [1024], replicated
- grad_shift_one: float32 [1024], replicated
- grad_w_in: float32 [1024, 4096], P('dp', 'tensor')
- grad_b_in: float32 [4096], P('tensor')
- grad_w_back: float32 [4096, 1024], P('tensor', 'dp')
- grad_b_back: float32 [1024], replicated
- grad_gain_two: float32 [1024], replicated
- grad_shift_two: float32 [1024], replicated
Inputs may be any that keep to these rules, and one draw needn't show every extreme that they name: The first lengths[s] slots of sequence s are real tokens; one sequence has 1024 and another 1024 // 4.
All inputs are finite; a program needn't handle non-finite values.
Results may differ from a plain program's by a relative error of at most 0.015.
The roundings to bfloat16 on the way count: a program that leaves them out, or rounds other values in their place, can miss the bound.
Values may be sent and summed in bfloat16 or wider, within the bound.
A program may use at most 192 MiB of HBM per device.

v0:
```python
from functools import partial
import jax
import jax.numpy as jnp
from jax import lax
from jax.sharding import PartitionSpec as P

HD = 64
EPSILON = 1e-05
NEGATIVE = -1e30


def norm_rows(values, norm_gain, norm_shift):
    average = jnp.mean(values, axis=-1, keepdims=True)
    centered = values - average
    variance = jnp.mean(centered * centered, axis=-1, keepdims=True)
    return centered * lax.rsqrt(variance + EPSILON) * norm_gain + norm_shift


def gelu_exact(values):
    return jax.nn.gelu(values, approximate=False)


def contract_rows(left_side, right_side):
    return lax.dot_general(
        left_side, right_side, (((0,), (0,)), ((), ())), preferred_element_type=jnp.float32
    )


def contract_cols(left_side, right_side):
    return lax.dot_general(
        left_side, right_side, (((1,), (1,)), ((), ())), preferred_element_type=jnp.float32
    )


def attend_forward(query_rows, key_rows, value_rows, key_valid):
    scores = jnp.einsum("qhd,khd->hqk", query_rows, key_rows, preferred_element_type=jnp.float32)
    scores = jnp.where(key_valid[None, None, :], scores, NEGATIVE)
    largest = jnp.max(scores, axis=-1, keepdims=True)
    weights = jnp.exp(scores - largest)
    row_total = jnp.sum(weights, axis=-1, keepdims=True)
    chances = (weights / row_total).astype(jnp.bfloat16)
    context = jnp.einsum("hqk,khd->qhd", chances, value_rows, preferred_element_type=jnp.float32)
    return (context, largest[:, :, 0] + jnp.log(row_total[:, :, 0]))


def attend_backward(log_total, grad_context, query_rows, key_rows, value_rows, key_valid):
    scores = jnp.einsum("qhd,khd->hqk", query_rows, key_rows, preferred_element_type=jnp.float32)
    scores = jnp.where(key_valid[None, None, :], scores, NEGATIVE)
    chances = jnp.exp(scores - log_total[:, :, None])
    grad_values = jnp.einsum(
        "hqk,qhd->khd",
        chances.astype(jnp.bfloat16),
        grad_context,
        preferred_element_type=jnp.float32,
    )
    grad_chances = jnp.einsum(
        "qhd,khd->hqk", grad_context, value_rows, preferred_element_type=jnp.float32
    )
    inner = jnp.sum(grad_chances * chances, axis=-1, keepdims=True)
    grad_scores = (chances * (grad_chances - inner)).astype(jnp.bfloat16)
    grad_queries = jnp.einsum(
        "hqk,khd->qhd", grad_scores, key_rows, preferred_element_type=jnp.float32
    )
    grad_keys = jnp.einsum(
        "hqk,qhd->khd", grad_scores, query_rows, preferred_element_type=jnp.float32
    )
    return (grad_queries, grad_keys, grad_values)


def fetch_weights(w_query, w_key, w_value, w_in, w_out, w_back):
    gathered_rows = (
        lax.all_gather(w_query, "dp", axis=0, tiled=True),
        lax.all_gather(w_key, "dp", axis=0, tiled=True),
        lax.all_gather(w_value, "dp", axis=0, tiled=True),
        lax.all_gather(w_in, "dp", axis=0, tiled=True),
    )
    gathered_columns = (
        lax.all_gather(w_out, "dp", axis=1, tiled=True),
        lax.all_gather(w_back, "dp", axis=1, tiled=True),
    )
    joined = jnp.concatenate([gathered_rows[0], gathered_rows[1], gathered_rows[2]], axis=1)
    return (joined, gathered_rows[3], gathered_columns[0], gathered_columns[1])


def on_device(
    inputs,
    lengths,
    w_query,
    w_key,
    w_value,
    b_query,
    b_value,
    w_out,
    b_out,
    gain_one,
    shift_one,
    w_in,
    b_in,
    w_back,
    b_back,
    gain_two,
    shift_two,
    cotangent,
):
    f32 = jnp.float32
    bf16 = jnp.bfloat16
    tensor_size = lax.axis_size("tensor")
    rows_here = inputs.shape[1]
    slots = rows_here * tensor_size
    local_width = w_query.shape[1]
    local_hidden = w_in.shape[1]
    local_heads = local_width // HD
    query_scale = HD ** (-0.5)
    block_rows = min(512, slots)
    row_place = lax.axis_index("tensor") * rows_here + jnp.arange(rows_here)
    query_bias = b_query.astype(f32)
    value_bias = b_value.astype(f32)
    out_bias = b_out.astype(f32)
    in_bias = b_in.astype(f32)
    back_bias = b_back.astype(f32)
    gain_first = gain_one.astype(f32)
    shift_first = shift_one.astype(f32)
    gain_second = gain_two.astype(f32)
    shift_second = shift_two.astype(f32)

    def one_batch(totals_now, batch_item):
        own_rows, length, grad_own = batch_item
        joined, matrix_in, matrix_out, matrix_back = fetch_weights(
            w_query, w_key, w_value, w_in, w_out, w_back
        )
        row_valid = row_place < length
        key_valid = jnp.arange(slots) < length
        full_in = lax.all_gather(own_rows, "tensor", axis=0, tiled=True)
        projected = jnp.dot(full_in, joined, preferred_element_type=f32)
        query_all = ((projected[:, :local_width] + query_bias) * query_scale).astype(bf16)
        key_all = projected[:, local_width : 2 * local_width].astype(bf16)
        value_all = (projected[:, 2 * local_width :] + value_bias).astype(bf16)
        query_heads = query_all.reshape(slots, local_heads, HD)
        key_heads = key_all.reshape(slots, local_heads, HD)
        value_heads = value_all.reshape(slots, local_heads, HD)
        context_blocks = []
        log_blocks = []
        for row_start in range(0, slots, block_rows):
            query_block = query_heads[row_start : row_start + block_rows]
            produced = attend_forward(query_block, key_heads, value_heads, key_valid)
            context_blocks.append(produced[0])
            log_blocks.append(produced[1])
        context_low = (
            jnp.concatenate(context_blocks, axis=0).reshape(slots, local_width).astype(bf16)
        )
        log_total = jnp.concatenate(log_blocks, axis=1)
        attended = lax.psum_scatter(
            jnp.dot(context_low, matrix_out, preferred_element_type=f32),
            "tensor",
            scatter_dimension=0,
            tiled=True,
        )
        first_sum = own_rows.astype(f32) + attended + out_bias
        first_norm, first_back = jax.vjp(norm_rows, first_sum, gain_first, shift_first)
        first_low = first_norm.astype(bf16)
        full_first = lax.all_gather(first_low, "tensor", axis=0, tiled=True)
        pre_act = jnp.dot(full_first, matrix_in, preferred_element_type=f32) + in_bias
        activated, gelu_back = jax.vjp(gelu_exact, pre_act)
        hidden_low = activated.astype(bf16)
        mixed_rows = lax.psum_scatter(
            jnp.dot(hidden_low, matrix_back, preferred_element_type=f32),
            "tensor",
            scatter_dimension=0,
            tiled=True,
        )
        second_sum = first_norm + mixed_rows + back_bias
        second, second_back = jax.vjp(norm_rows, second_sum, gain_second, shift_second)
        layer_rows = jnp.where(row_valid[:, None], second, 0.0).astype(bf16)
        joined, matrix_in, matrix_out, matrix_back = fetch_weights(
            w_query, w_key, w_value, w_in, w_out, w_back
        )
        grad_second = jnp.where(row_valid[:, None], grad_own.astype(f32), 0.0)
        grad_mixed, grad_gain_b, grad_shift_b = second_back(grad_second)
        full_grad_mixed = lax.all_gather(grad_mixed.astype(bf16), "tensor", axis=0, tiled=True)
        grad_activated = contract_cols(full_grad_mixed, matrix_back)
        grad_back_w = contract_rows(hidden_low, full_grad_mixed)
        (grad_pre,) = gelu_back(grad_activated)
        grad_pre_low = grad_pre.astype(bf16)
        grad_in_bias = jnp.sum(grad_pre_low.astype(f32), axis=0)
        grad_in_w = contract_rows(full_first, grad_pre_low)
        grad_first_mix = lax.psum_scatter(
            contract_cols(grad_pre_low, matrix_in), "tensor", scatter_dimension=0, tiled=True
        )
        grad_first = grad_mixed + grad_first_mix
        grad_att, grad_gain_a, grad_shift_a = first_back(grad_first)
        full_grad_att = lax.all_gather(grad_att.astype(bf16), "tensor", axis=0, tiled=True)
        grad_context = contract_cols(full_grad_att, matrix_out).astype(bf16)
        grad_out_w = contract_rows(context_low, full_grad_att)
        grad_context_heads = grad_context.reshape(slots, local_heads, HD)
        query_grad_blocks = []
        key_grad_sum = jnp.zeros((slots, local_heads, HD), f32)
        value_grad_sum = jnp.zeros((slots, local_heads, HD), f32)
        for row_start in range(0, slots, block_rows):
            query_block = query_heads[row_start : row_start + block_rows]
            block_fn = partial(
                attend_backward,
                log_total[:, row_start : row_start + block_rows],
                grad_context_heads[row_start : row_start + block_rows],
            )
            produced = block_fn(query_block, key_heads, value_heads, key_valid)
            query_grad_blocks.append(produced[0])
            key_grad_sum = key_grad_sum + produced[1]
            value_grad_sum = value_grad_sum + produced[2]
        grad_query_low = (
            jnp.concatenate(query_grad_blocks, axis=0).reshape(slots, local_width).astype(bf16)
        )
        grad_key_low = key_grad_sum.reshape(slots, local_width).astype(bf16)
        grad_value_low = value_grad_sum.reshape(slots, local_width).astype(bf16)
        grad_projected = jnp.concatenate(
            [grad_query_low * query_scale, grad_key_low, grad_value_low], axis=1
        )
        grad_joined_w = contract_rows(full_in, grad_projected)
        grad_query_bias = jnp.sum(grad_projected[:, :local_width].astype(f32), axis=0)
        grad_value_bias = jnp.sum(grad_value_low.astype(f32), axis=0)
        grad_input_mix = lax.psum_scatter(
            contract_cols(grad_projected, joined).astype(jnp.bfloat16),
            "tensor",
            scatter_dimension=0,
            tiled=True,
        ).astype(jnp.float32)
        grad_rows = grad_att + grad_input_mix
        increments = (
            grad_joined_w,
            grad_out_w,
            grad_in_w,
            grad_back_w,
            grad_query_bias,
            grad_value_bias,
            grad_in_bias,
            jnp.sum(grad_att, axis=0),
            grad_gain_a,
            grad_shift_a,
            jnp.sum(grad_mixed, axis=0),
            grad_gain_b,
            grad_shift_b,
        )
        totals_next = jax.tree.map(jnp.add, totals_now, increments)
        return (totals_next, (layer_rows, grad_rows))

    model_width = w_out.shape[1] * lax.axis_size("dp")
    starting = (
        jnp.zeros((model_width, 3 * local_width), f32),
        jnp.zeros((local_width, model_width), f32),
        jnp.zeros((model_width, local_hidden), f32),
        jnp.zeros((local_hidden, model_width), f32),
        jnp.zeros((local_width,), f32),
        jnp.zeros((local_width,), f32),
        jnp.zeros((local_hidden,), f32),
        jnp.zeros((model_width,), f32),
        jnp.zeros((model_width,), f32),
        jnp.zeros((model_width,), f32),
        jnp.zeros((model_width,), f32),
        jnp.zeros((model_width,), f32),
        jnp.zeros((model_width,), f32),
    )
    totals, stacked = lax.scan(one_batch, starting, (inputs, lengths, cotangent))
    layer_out, grad_inputs = stacked
    grad_joined_w = totals[0]
    reduced_rows = (
        lax.psum_scatter(grad_joined_w[:, :local_width], "dp", scatter_dimension=0, tiled=True),
        lax.psum_scatter(
            grad_joined_w[:, local_width : 2 * local_width], "dp", scatter_dimension=0, tiled=True
        ),
        lax.psum_scatter(
            grad_joined_w[:, 2 * local_width :], "dp", scatter_dimension=0, tiled=True
        ),
        lax.psum_scatter(totals[2], "dp", scatter_dimension=0, tiled=True),
    )
    reduced_columns = (
        lax.psum_scatter(totals[1], "dp", scatter_dimension=1, tiled=True),
        lax.psum_scatter(totals[3], "dp", scatter_dimension=1, tiled=True),
    )
    bias_sums = lax.psum((totals[4], totals[5], totals[6]), "dp")
    norm_sums = lax.psum(
        (totals[7], totals[8], totals[9], totals[10], totals[11], totals[12]), ("dp", "tensor")
    )
    return (
        layer_out,
        grad_inputs,
        reduced_rows[0],
        reduced_rows[1],
        reduced_rows[2],
        bias_sums[0],
        bias_sums[1],
        reduced_columns[0],
        norm_sums[0],
        norm_sums[1],
        norm_sums[2],
        reduced_rows[3],
        bias_sums[2],
        reduced_columns[1],
        norm_sums[3],
        norm_sums[4],
        norm_sums[5],
    )


def solution(mesh):
    return jax.shard_map(
        on_device,
        mesh=mesh,
        in_specs=(
            P("dp", "tensor", None),
            P("dp"),
            P("dp", "tensor"),
            P("dp", "tensor"),
            P("dp", "tensor"),
            P("tensor"),
            P("tensor"),
            P("tensor", "dp"),
            P(),
            P(),
            P(),
            P("dp", "tensor"),
            P("tensor"),
            P("tensor", "dp"),
            P(),
            P(),
            P(),
            P("dp", "tensor", None),
        ),
        out_specs=(
            P("dp", "tensor", None),
            P("dp", "tensor", None),
            P("dp", "tensor"),
            P("dp", "tensor"),
            P("dp", "tensor"),
            P("tensor"),
            P("tensor"),
            P("tensor", "dp"),
            P(),
            P(),
            P(),
            P("dp", "tensor"),
            P("tensor"),
            P("tensor", "dp"),
            P(),
            P(),
            P(),
        ),
        check_vma=False,
    )
```

profile of v0, /device:TPU:0, one launch (start us, length us, event | category | flops | bytes accessed | tf_op | source)
XLA Modules:
  0.0 1471.8 jit_solution(11094318295025059923)
XLA Ops:
  14.3 1180.0 %while.39 = (s32[]{:T(128)}, f32[1024,768]{1,0:T(8,128)}, f32[256,1024]{1,0:T(8,128)}, f32[1024,1024]{1,0:T(8,128)}, f32[1024,1024]{1,0:T(8,128)}, /*index=5*/f3...) while((s32[]{:T(128)}, f32[1024,768]{1,0:T(8,128)}, ...), condition=%wide.region_28.29_spmd.clone, body=%wide.region_0.28_spmd.clone.sunk | while | flops 22766163968 | bytes 654625408 | solution.py:261
  18.1 11.7 all_gather.57
  29.8 9.5 all_gather.56
  48.6 9.5 all_gather.54
  85.5 75.0 %reduce-scatter.23.cloned.1.call-done = f32[256,1024]{1,0:T(8,128)} async-done(((f32[1024,1024]{1,0:T(8,128)}), f32[256,1024]{1,0:T(8,128)}) %reduce-scatter.23.cloned.1.call-update) | async-done | bytes 1048592 | tf_op jit(solution)/shard_map/while/body/eval_jaxpr/reduce_scatter | solution.py:152
  164.5 45.0 %all-gather.13.cloned.1.call-done = bf16[1024,1024]{1,0:T(8,128)(2,1)} async-done(((bf16[256,1024]{1,0:T(8,128)(2,1)}), bf16[1024,1024]{1,0:T(8,128)(2,1)}) %all-gather.13.cloned.1.call-update) | async-done | bytes 2097168 | tf_op jit(solution)/shard_map/while/body/eval_jaxpr/all_gather | solution.py:161
  209.5 14.9 %multiply_convert_fusion.5 = (bf16[1024,1024]{1,0:T(8,128)(2,1)}, f32[1024,1024]{1,0:T(8,128)}, f32[1024,1024]{1,0:T(8,128)}) fusion(f32[1024]{0:T(1024)S(1)} %get-tuple-element.881, bf16[1024,1024]{1,0:T(8,128)(2,1)} %all-gather.13.cloned.1.call-done, bf16[1024,1024]{1,0:T(8,128)(2,1)} %all-gather.15.cloned.1.call-done), kind=kOutput, calls=%fused_computation.26.clone.1 | convolution fusion | flops 2216689664 | bytes 14684160 | tf_op jit(solution)/shard_map/while/body/eval_jaxpr/dot_general | solution.py:162
  224.4 13.8 all-gather.17.cloned.1.call-done
  245.6 76.2 %reduce-scatter.25.cloned.1.call-done = f32[256,1024]{1,0:T(8,128)} async-done(((f32[1024,1024]{1,0:T(8,128)}), f32[256,1024]{1,0:T(8,128)}) %reduce-scatter.25.cloned.1.call-update) | async-done | bytes 1048592 | tf_op jit(solution)/shard_map/while/body/eval_jaxpr/reduce_scatter | solution.py:165
  330.0 46.5 %all-gather.19.cloned.1.call-done = bf16[1024,1024]{1,0:T(8,128)(2,1)} async-done(((bf16[256,1024]{1,0:T(8,128)(2,1)}), bf16[1024,1024]{1,0:T(8,128)(2,1)}) %all-gather.19.cloned.1.call-update) | async-done | bytes 2097168 | tf_op jit(solution)/shard_map/while/body/eval_jaxpr/all_gather | solution.py:179
  390.7 75.6 %reduce-scatter.27.cloned.1.call-done = f32[256,1024]{1,0:T(8,128)} async-done(((f32[1024,1024]{1,0:T(8,128)}), f32[256,1024]{1,0:T(8,128)}) %reduce-scatter.27.cloned.1.call-update) | async-done | bytes 1048592 | tf_op jit(solution)/shard_map/while/body/eval_jaxpr/reduce_scatter | solution.py:186
  471.0 45.9 %all-gather.21.cloned.1.call-done = bf16[1024,1024]{1,0:T(8,128)(2,1)} async-done(((bf16[256,1024]{1,0:T(8,128)(2,1)}), bf16[1024,1024]{1,0:T(8,128)(2,1)}) %all-gather.21.cloned.1.call-update) | async-done | bytes 2097168 | tf_op jit(solution)/shard_map/while/body/eval_jaxpr/all_gather | solution.py:191
  578.3 24.3 %reduce-scatter.29.cloned.1.call-done = bf16[256,1024]{1,0:T(8,128)(2,1)} async-done(((bf16[1024,1024]{1,0:T(8,128)(2,1)}), bf16[256,1024]{1,0:T(8,128)(2,1)}) %reduce-scatter.29.cloned.1.call-update) | async-done | bytes 524304 | tf_op jit(solution)/shard_map/while/body/eval_jaxpr/reduce_scatter | solution.py:220
  609.1 10.2 all_gather.57
  619.3 9.5 all_gather.56
  638.1 9.5 all_gather.54
  672.7 75.0 %reduce-scatter.23.cloned.1.call-done = f32[256,1024]{1,0:T(8,128)} async-done(((f32[1024,1024]{1,0:T(8,128)}), f32[256,1024]{1,0:T(8,128)}) %reduce-scatter.23.cloned.1.call-update) | async-done | bytes 1048592 | tf_op jit(solution)/shard_map/while/body/eval_jaxpr/reduce_scatter | solution.py:152
  751.3 45.4 %all-gather.13.cloned.1.call-done = bf16[1024,1024]{1,0:T(8,128)(2,1)} async-done(((bf16[256,1024]{1,0:T(8,128)(2,1)}), bf16[1024,1024]{1,0:T(8,128)(2,1)}) %all-gather.13.cloned.1.call-update) | async-done | bytes 2097168 | tf_op jit(solution)/shard_map/while/body/eval_jaxpr/all_gather | solution.py:161
  796.7 14.9 %multiply_convert_fusion.5 = (bf16[1024,1024]{1,0:T(8,128)(2,1)}, f32[1024,1024]{1,0:T(8,128)}, f32[1024,1024]{1,0:T(8,128)}) fusion(f32[1024]{0:T(1024)S(1)} %get-tuple-element.881, bf16[1024,1024]{1,0:T(8,128)(2,1)} %all-gather.13.cloned.1.call-done, bf16[1024,1024]{1,0:T(8,128)(2,1)} %all-gather.15.cloned.1.call-done), kind=kOutput, calls=%fused_computation.26.clone.1 | convolution fusion | flops 2216689664 | bytes 14684160 | tf_op jit(solution)/shard_map/while/body/eval_jaxpr/dot_general | solution.py:162
  811.6 13.8 all-gather.17.cloned.1.call-done
  832.8 76.2 %reduce-scatter.25.cloned.1.call-done = f32[256,1024]{1,0:T(8,128)} async-done(((f32[1024,1024]{1,0:T(8,128)}), f32[256,1024]{1,0:T(8,128)}) %reduce-scatter.25.cloned.1.call-update) | async-done | bytes 1048592 | tf_op jit(solution)/shard_map/while/body/eval_jaxpr/reduce_scatter | solution.py:165
  917.2 46.5 %all-gather.19.cloned.1.call-done = bf16[1024,1024]{1,0:T(8,128)(2,1)} async-done(((bf16[256,1024]{1,0:T(8,128)(2,1)}), bf16[1024,1024]{1,0:T(8,128)(2,1)}) %all-gather.19.cloned.1.call-update) | async-done | bytes 2097168 | tf_op jit(solution)/shard_map/while/body/eval_jaxpr/all_gather | solution.py:179
  977.9 75.6 %reduce-scatter.27.cloned.1.call-done = f32[256,1024]{1,0:T(8,128)} async-done(((f32[1024,1024]{1,0:T(8,128)}), f32[256,1024]{1,0:T(8,128)}) %reduce-scatter.27.cloned.1.call-update) | async-done | bytes 1048592 | tf_op jit(solution)/shard_map/while/body/eval_jaxpr/reduce_scatter | solution.py:186
  1058.3 45.9 %all-gather.21.cloned.1.call-done = bf16[1024,1024]{1,0:T(8,128)(2,1)} async-done(((bf16[256,1024]{1,0:T(8,128)(2,1)}), bf16[1024,1024]{1,0:T(8,128)(2,1)}) %all-gather.21.cloned.1.call-update) | async-done | bytes 2097168 | tf_op jit(solution)/shard_map/while/body/eval_jaxpr/all_gather | solution.py:191
  1172.2 17.8 %reduce-scatter.29.cloned.1.call-done = bf16[256,1024]{1,0:T(8,128)(2,1)} async-done(((bf16[1024,1024]{1,0:T(8,128)(2,1)}), bf16[256,1024]{1,0:T(8,128)(2,1)}) %reduce-scatter.29.cloned.1.call-update) | async-done | bytes 524304 | tf_op jit(solution)/shard_map/while/body/eval_jaxpr/reduce_scatter | solution.py:220
  1201.3 14.1 all-reduce.1
  1215.4 39.5 %all-reduce = (f32[1024]{0:T(1024)}, f32[1024]{0:T(1024)}, f32[1024]{0:T(1024)}, f32[1024]{0:T(1024)}, f32[1024]{0:T(1024)}, /*index=5*/f32[1024]{0:T(1024)}) all-reduce(f32[1024]{0:T(1024)S(1)} %copy-done.28, f32[1024]{0:T(1024)S(1)} %copy-done.25, f32[1024]{0:T(1024)S(1)} %copy-done.22, ...), channel_id=1, replica_groups=mesh['dp'=8,'tensor'=4] {'dp','tensor'}, use_global_device_ids=true, to_apply=%region_35.36 | all-reduce | flops 6144 | bytes 49152 | tf_op jit(solution)/shard_map/psum | solution.py:279
  1254.9 19.2 %reduce-scatter.15.cloned.1.call-done = f32[128,256]{1,0:T(8,128)} async-done(((f32[1024,256]{1,0:T(8,128)}), f32[128,256]{1,0:T(8,128)}) %reduce-scatter.15.cloned.1.call-update) | async-done | bytes 131088 | tf_op jit(solution)/shard_map/reduce_scatter | solution.py:269
  1274.1 39.8 %reduce-scatter.11.cloned.1.call-done = f32[128,256]{1,0:T(8,128)} async-done(((f32[1024,256]{1,0:T(8,128)}), f32[128,256]{1,0:T(8,128)}) %reduce-scatter.11.cloned.1.call-update) | async-done | bytes 131088 | tf_op jit(solution)/shard_map/reduce_scatter | solution.py:265
  1313.9 39.7 %reduce-scatter.13.cloned.1.call-done = f32[128,256]{1,0:T(8,128)} async-done(((f32[1024,256]{1,0:T(8,128)}), f32[128,256]{1,0:T(8,128)}) %reduce-scatter.13.cloned.1.call-update) | async-done | bytes 131088 | tf_op jit(solution)/shard_map/reduce_scatter | solution.py:266
  1353.6 55.3 %reduce-scatter.19.cloned.1.call-done = f32[128,1024]{1,0:T(8,128)} async-done(((f32[1024,1024]{1,0:T(8,128)}), f32[128,1024]{1,0:T(8,128)}) %reduce-scatter.19.cloned.1.call-update) | async-done | bytes 524304 | tf_op jit(solution)/shard_map/reduce_scatter | solution.py:272
  1408.9 55.5 %reduce-scatter.21.cloned.1.call-done = f32[1024,128]{1,0:T(8,128)} async-done(((f32[1024,1024]{1,0:T(8,128)}), f32[1024,128]{1,0:T(8,128)}) %reduce-scatter.21.cloned.1.call-update) | async-done | bytes 524304 | tf_op jit(solution)/shard_map/reduce_scatter | solution.py:276
  (400 shorter events, 300.7 us)
Async XLA Ops:
  14.3 51.6 %all-gather.11.cloned.1.call-start = ((), (), s32[]{:S(2)}) async-start(), calls=%async_computation.16 | async-start | bytes 2621440 | tf_op jit(solution)/shard_map/while/body/eval_jaxpr/all_gather | solution.py:133
  16.2 144.3 %reduce-scatter.23.cloned.1.call-start = ((), (), s32[]{:S(2)}) async-start(), calls=%async_computation.17 | async-start | bytes 5242880 | tf_op jit(solution)/shard_map/while/body/eval_jaxpr/reduce_scatter | solution.py:152
  29.8 52.3 %copy-start.12 = (bf16[256,1024]{1,0:T(8,128)(2,1)}, bf16[256,1024]{1,0:T(8,128)(2,1)S(1)}, u32[]{:S(2)}) copy-start(bf16[256,1024]{1,0:T(8,128)(2,1)S(1)} %all_gather.57) | copy-start | bytes 1572868 | tf_op jit(solution)/shard_map/while
  84.8 75.7 %copy-start.13 = (bf16[2,256,1024]{2,1,0:T(8,128)(2,1)S(1)}, bf16[2,256,1024]{2,1,0:T(8,128)(2,1)}, u32[]{:S(2)}) copy-start(bf16[2,256,1024]{2,1,0:T(8,128)(2,1)} %get-tuple-element.867) | copy-start | bytes 3145732 | tf_op jit(solution)/shard_map/while
  84.9 79.6 %all-gather.15.cloned.1.call-start = ((), (), s32[]{:S(2)}) async-start(), calls=%async_computation.19 | async-start | bytes 2359296 | tf_op jit(solution)/shard_map/while/body/eval_jaxpr/all_gather | solution.py:75
  85.4 124.0 %all-gather.13.cloned.1.call-start = ((), (), s32[]{:S(2)}) async-start(), calls=%async_computation.18 | async-start | bytes 2621440 | tf_op jit(solution)/shard_map/while/body/eval_jaxpr/all_gather | solution.py:161
  163.3 74.9 %all-gather.17.cloned.1.call-start = ((), (), s32[]{:S(2)}) async-start(), calls=%async_computation.20 | async-start | bytes 2359296 | tf_op jit(solution)/shard_map/while/body/eval_jaxpr/all_gather | solution.py:79
  163.9 157.9 %reduce-scatter.25.cloned.1.call-start = ((), (), s32[]{:S(2)}) async-start(), calls=%async_computation.21 | async-start | bytes 5242880 | tf_op jit(solution)/shard_map/while/body/eval_jaxpr/reduce_scatter | solution.py:165
  244.9 131.5 %all-gather.19.cloned.1.call-start = ((), (), s32[]{:S(2)}) async-start(), calls=%async_computation.22 | async-start | bytes 2621440 | tf_op jit(solution)/shard_map/while/body/eval_jaxpr/all_gather | solution.py:179
  329.9 136.4 %reduce-scatter.27.cloned.1.call-start = ((), (), s32[]{:S(2)}) async-start(), calls=%async_computation.23 | async-start | bytes 5242880 | tf_op jit(solution)/shard_map/while/body/eval_jaxpr/reduce_scatter | solution.py:186
  390.7 126.3 %all-gather.21.cloned.1.call-start = ((), (), s32[]{:S(2)}) async-start(), calls=%async_computation.24 | async-start | bytes 2621440 | tf_op jit(solution)/shard_map/while/body/eval_jaxpr/all_gather | solution.py:191
  470.8 131.8 %reduce-scatter.29.cloned.1.call-start = ((), (), s32[]{:S(2)}) async-start(), calls=%async_computation.25 | async-start | bytes 2621440 | tf_op jit(solution)/shard_map/while/body/eval_jaxpr/reduce_scatter | solution.py:220
  574.8 27.8 %copy-start.3 = (f32[256,1024]{1,0:T(8,128)S(1)}, f32[256,1024]{1,0:T(8,128)}, u32[]{:S(2)}) copy-start(f32[256,1024]{1,0:T(8,128)} %copy-done.2) | copy-start | bytes 3145732 | tf_op jit(solution)/shard_map/while
  605.2 47.9 %all-gather.11.cloned.1.call-start = ((), (), s32[]{:S(2)}) async-start(), calls=%async_computation.16 | async-start | bytes 2621440 | tf_op jit(solution)/shard_map/while/body/eval_jaxpr/all_gather | solution.py:133
  607.2 140.5 %reduce-scatter.23.cloned.1.call-start = ((), (), s32[]{:S(2)}) async-start(), calls=%async_computation.17 | async-start | bytes 5242880 | tf_op jit(solution)/shard_map/while/body/eval_jaxpr/reduce_scatter | solution.py:152
  619.3 50.0 %copy-start.12 = (bf16[256,1024]{1,0:T(8,128)(2,1)}, bf16[256,1024]{1,0:T(8,128)(2,1)S(1)}, u32[]{:S(2)}) copy-start(bf16[256,1024]{1,0:T(8,128)(2,1)S(1)} %all_gather.57) | copy-start | bytes 1572868 | tf_op jit(solution)/shard_map/while
  672.0 75.7 %copy-start.13 = (bf16[2,256,1024]{2,1,0:T(8,128)(2,1)S(1)}, bf16[2,256,1024]{2,1,0:T(8,128)(2,1)}, u32[]{:S(2)}) copy-start(bf16[2,256,1024]{2,1,0:T(8,128)(2,1)} %get-tuple-element.867) | copy-start | bytes 3145732 | tf_op jit(solution)/shard_map/while
  672.1 79.3 %all-gather.15.cloned.1.call-start = ((), (), s32[]{:S(2)}) async-start(), calls=%async_computation.19 | async-start | bytes 2359296 | tf_op jit(solution)/shard_map/while/body/eval_jaxpr/all_gather | solution.py:75
  672.7 124.0 %all-gather.13.cloned.1.call-start = ((), (), s32[]{:S(2)}) async-start(), calls=%async_computation.18 | async-start | bytes 2621440 | tf_op jit(solution)/shard_map/while/body/eval_jaxpr/all_gather | solution.py:161
  750.5 74.9 %all-gather.17.cloned.1.call-start = ((), (), s32[]{:S(2)}) async-start(), calls=%async_computation.20 | async-start | bytes 2359296 | tf_op jit(solution)/shard_map/while/body/eval_jaxpr/all_gather | solution.py:79
  751.1 157.9 %reduce-scatter.25.cloned.1.call-start = ((), (), s32[]{:S(2)}) async-start(), calls=%async_computation.21 | async-start | bytes 5242880 | tf_op jit(solution)/shard_map/while/body/eval_jaxpr/reduce_scatter | solution.py:165
  832.1 131.5 %all-gather.19.cloned.1.call-start = ((), (), s32[]{:S(2)}) async-start(), calls=%async_computation.22 | async-start | bytes 2621440 | tf_op jit(solution)/shard_map/while/body/eval_jaxpr/all_gather | solution.py:179
  917.1 136.4 %reduce-scatter.27.cloned.1.call-start = ((), (), s32[]{:S(2)}) async-start(), calls=%async_computation.23 | async-start | bytes 5242880 | tf_op jit(solution)/shard_map/while/body/eval_jaxpr/reduce_scatter | solution.py:186
  977.9 126.3 %all-gather.21.cloned.1.call-start = ((), (), s32[]{:S(2)}) async-start(), calls=%async_computation.24 | async-start | bytes 2621440 | tf_op jit(solution)/shard_map/while/body/eval_jaxpr/all_gather | solution.py:191
  1058.0 132.0 %reduce-scatter.29.cloned.1.call-start = ((), (), s32[]{:S(2)}) async-start(), calls=%async_computation.25 | async-start | bytes 2621440 | tf_op jit(solution)/shard_map/while/body/eval_jaxpr/reduce_scatter | solution.py:220
  1166.6 23.4 %copy-start.3 = (f32[256,1024]{1,0:T(8,128)S(1)}, f32[256,1024]{1,0:T(8,128)}, u32[]{:S(2)}) copy-start(f32[256,1024]{1,0:T(8,128)} %copy-done.2) | copy-start | bytes 3145732 | tf_op jit(solution)/shard_map/while
  1194.3 60.7 %reduce-scatter.17.cloned.1.call-start = ((), (), s32[]{:S(2)}) async-start(), calls=%async_computation.13 | async-start | bytes 1179648 | tf_op jit(solution)/shard_map/reduce_scatter | solution.py:275
  1195.0 79.1 %reduce-scatter.15.cloned.1.call-start = ((), (), s32[]{:S(2)}) async-start(), calls=%async_computation.12 | async-start | bytes 1179648 | tf_op jit(solution)/shard_map/reduce_scatter | solution.py:269
  1198.7 115.3 %reduce-scatter.11.cloned.1.call-start = ((), (), s32[]{:S(2)}) async-start(), calls=%async_computation.10 | async-start | bytes 1179648 | tf_op jit(solution)/shard_map/reduce_scatter | solution.py:265
  1199.4 154.2 %reduce-scatter.13.cloned.1.call-start = ((), (), s32[]{:S(2)}) async-start(), calls=%async_computation.11 | async-start | bytes 1179648 | tf_op jit(solution)/shard_map/reduce_scatter | solution.py:266
  1200.0 208.9 %reduce-scatter.19.cloned.1.call-start = ((), (), s32[]{:S(2)}) async-start(), calls=%async_computation.14 | async-start | bytes 4718592 | tf_op jit(solution)/shard_map/reduce_scatter | solution.py:272
  1200.7 263.7 %reduce-scatter.21.cloned.1.call-start = ((), (), s32[]{:S(2)}) async-start(), calls=%async_computation.15 | async-start | bytes 4718592 | tf_op jit(solution)/shard_map/reduce_scatter | solution.py:276
  (81 other events, 480.7 us)
Sparse Core Ops, SparseCore 0:
  17.2 48.6 all-gather.10
  85.0 75.4 reduce-scatter.22
  330.1 46.3 all-gather.18
  390.8 75.4 reduce-scatter.26
  607.9 45.1 all-gather.10
  672.2 75.4 reduce-scatter.22
  917.3 46.3 all-gather.18
  978.0 75.4 reduce-scatter.26
  1198.9 35.5 reduce-scatter.16
  1238.1 36.0 reduce-scatter.14
  1277.9 36.0 reduce-scatter.10
  1317.5 36.0 reduce-scatter.12
  1357.5 51.2 reduce-scatter.18
  1413.0 51.3 reduce-scatter.20
Sparse Core Ops, SparseCore 1:
  87.2 26.4 all-gather.14
  163.4 46.0 all-gather.12
  211.4 26.8 all-gather.16
  245.0 76.7 reduce-scatter.24
  470.9 46.0 all-gather.20
  560.3 42.3 reduce-scatter.28
  674.4 26.4 all-gather.14
  750.6 46.0 all-gather.12
  798.6 26.8 all-gather.16
  832.2 76.7 reduce-scatter.24
  1058.1 46.0 all-gather.20
  1147.7 42.3 reduce-scatter.28
where the time goes:
time: 1470 us
  waiting for transfers between devices  1030 us (70%)
  matrix products  206 us (14%)
  blocking collectives  132 us (9%)
  other arithmetic  63.6 us (4%)
  local copies, waits for them, and re-layouts  21.4 us (1%)
  between operations  15.7 us (1%)
    reduce_scatter x2, waiting for transfers between devices, one_batch(): lax.psum_scatter(jnp.dot(hidden_low, matrix_back, preferred_element_type=...  152 us
    reduce_scatter x2, waiting for transfers between devices, one_batch(): lax.psum_scatter(contract_cols(grad_pre_low, matrix_in), 'tensor', scatte...  151 us
    reduce_scatter x2, waiting for transfers between devices, one_batch(): lax.psum_scatter(jnp.dot(context_low, matrix_out, preferred_element_type=...  150 us
    all_gather x2, waiting for transfers between devices, one_batch(): lax.all_gather(grad_mixed.astype(bf16), 'tensor', axis=0, tiled=True)  92.9 us
    all_gather x2, waiting for transfers between devices, one_batch(): lax.all_gather(grad_att.astype(bf16), 'tensor', axis=0, tiled=True)  91.8 us
    all_gather x2, waiting for transfers between devices, one_batch(): full_first = lax.all_gather(first_low, 'tensor', axis=0, tiled=True)  90.3 us
    reduce_scatter x1, waiting for transfers between devices, on_device(): lax.psum_scatter(totals[3], 'dp', scatter_dimension=1, tiled=True)  55.5 us
    reduce_scatter x1, waiting for transfers between devices, on_device(): lax.psum_scatter(totals[2], 'dp', scatter_dimension=0, tiled=True)  55.3 us
  transfers between devices with their start and end apart: 26, of which 23 were waited for; matrix products, arithmetic and copies ran while one was open for 6% of the time, Pallas kernels for 0%

commit v1 on v0

--- a/solution.py
+++ b/solution.py
@@ -188,7 +188,12 @@
         )
         grad_first = grad_mixed + grad_first_mix
         grad_att, grad_gain_a, grad_shift_a = first_back(grad_first)
-        full_grad_att = lax.all_gather(grad_att.astype(bf16), "tensor", axis=0, tiled=True)
+        full_grad_att = jnp.concatenate(
+            lax.all_to_all(
+                jnp.stack([grad_att.astype(bf16)] * lax.axis_size("tensor")), "tensor", 0, 0
+            ),
+            axis=0,
+        )
         grad_context = contract_cols(full_grad_att, matrix_out).astype(bf16)
         grad_out_w = contract_rows(context_low, full_grad_att)
         grad_context_heads = grad_context.reshape(slots, local_heads, HD)

time: 1470 us -> 1500 us (1.020)
    all_to_all x0 -> x2, waiting for transfers between devices: none -> 97.1 us  [one_batch(): lax.all_to_all(jnp.stack([grad_att.astype(bf16)] * lax.axis_size('tensor'...]
    all_gather x2 -> x0, waiting for transfers between devices: 91.8 us -> none  [one_batch(): lax.all_gather(grad_att.astype(bf16), 'tensor', axis=0, tiled=True)]
where the time goes in v1:
time: 1500 us
  waiting for transfers between devices  1020 us (68%)
  matrix products  213 us (14%)
  blocking collectives  132 us (9%)
  other arithmetic  66.2 us (4%)
  local copies, waits for them, and re-layouts  30 us (2%)
  between operations  16.2 us (1%)
    reduce_scatter x2, waiting for transfers between devices, one_batch(): lax.psum_scatter(jnp.dot(hidden_low, matrix_back, preferred_element_type=...  152 us
    reduce_scatter x2, waiting for transfers between devices, one_batch(): lax.psum_scatter(contract_cols(grad_pre_low, matrix_in), 'tensor', scatte...  151 us
    reduce_scatter x2, waiting for transfers between devices, one_batch(): lax.psum_scatter(jnp.dot(context_low, matrix_out, preferred_element_type=...  150 us
    all_to_all x2, waiting for transfers between devices, one_batch(): lax.all_to_all(jnp.stack([grad_att.astype(bf16)] * lax.axis_size('tensor'...  97.1 us
    all_gather x2, waiting for transfers between devices, one_batch(): lax.all_gather(grad_mixed.astype(bf16), 'tensor', axis=0, tiled=True)  92.1 us
    all_gather x2, waiting for transfers between devices, one_batch(): full_first = lax.all_gather(first_low, 'tensor', axis=0, tiled=True)  90.5 us
    reduce_scatter x1, waiting for transfers between devices, on_device(): lax.psum_scatter(totals[3], 'dp', scatter_dimension=1, tiled=True)  55.5 us
    reduce_scatter x1, waiting for transfers between devices, on_device(): lax.psum_scatter(totals[2], 'dp', scatter_dimension=0, tiled=True)  55.2 us
  transfers between devices with their start and end apart: 26, of which 23 were waited for; matrix products, arithmetic and copies ran while one was open for 6% of the time, Pallas kernels for 0%

profile of v1, /device:TPU:0, one launch (start us, length us, event | category | flops | bytes accessed | tf_op | source)
XLA Modules:
  0.0 1496.5 jit_solution(2582315591460883887)
XLA Ops:
  16.6 1202.5 %while.39 = (s32[]{:T(128)}, f32[1024,768]{1,0:T(8,128)}, f32[256,1024]{1,0:T(8,128)}, f32[1024,1024]{1,0:T(8,128)}, f32[1024,1024]{1,0:T(8,128)}, /*index=5*/f3...) while((s32[]{:T(128)}, f32[1024,768]{1,0:T(8,128)}, ...), condition=%wide.region_28.29_spmd.clone, body=%wide.region_0.28_spmd.clone.sunk | while | flops 22767212544 | bytes 648753792 | solution.py:266
  20.5 11.7 all_gather.52
  32.3 9.5 all_gather.51
  51.0 9.5 all_gather.49
  89.1 75.0 %reduce-scatter.23.cloned.1.call-done = f32[256,1024]{1,0:T(8,128)} async-done(((f32[1024,1024]{1,0:T(8,128)}), f32[256,1024]{1,0:T(8,128)}) %reduce-scatter.23.cloned.1.call-update) | async-done | bytes 1048592 | tf_op jit(solution)/shard_map/while/body/eval_jaxpr/reduce_scatter | solution.py:152
  168.0 45.2 %all-gather.12.cloned.1.call-done = bf16[1024,1024]{1,0:T(8,128)(2,1)} async-done(((bf16[256,1024]{1,0:T(8,128)(2,1)}), bf16[1024,1024]{1,0:T(8,128)(2,1)}) %all-gather.12.cloned.1.call-update) | async-done | bytes 2097168 | tf_op jit(solution)/shard_map/while/body/eval_jaxpr/all_gather | solution.py:161
  213.1 15.0 %multiply_convert_fusion.5 = (bf16[1024,1024]{1,0:T(8,128)(2,1)}, f32[1024,1024]{1,0:T(8,128)}, f32[1024,1024]{1,0:T(8,128)}) fusion(f32[1024]{0:T(1024)S(1)} %get-tuple-element.881, bf16[1024,1024]{1,0:T(8,128)(2,1)} %all-gather.12.cloned.1.call-done, bf16[1024,1024]{1,0:T(8,128)(2,1)} %all-gather.14.cloned.1.call-done), kind=kOutput, calls=%fused_computation.26.clone.1 | convolution fusion | flops 2216689664 | bytes 14684160 | tf_op jit(solution)/shard_map/while/body/eval_jaxpr/dot_general | solution.py:162
  228.2 13.7 all-gather.16.cloned.1.call-done
  249.3 76.2 %reduce-scatter.25.cloned.1.call-done = f32[256,1024]{1,0:T(8,128)} async-done(((f32[1024,1024]{1,0:T(8,128)}), f32[256,1024]{1,0:T(8,128)}) %reduce-scatter.25.cloned.1.call-update) | async-done | bytes 1048592 | tf_op jit(solution)/shard_map/while/body/eval_jaxpr/reduce_scatter | solution.py:165
  334.3 45.9 %all-gather.18.cloned.1.call-done = bf16[1024,1024]{1,0:T(8,128)(2,1)} async-done(((bf16[256,1024]{1,0:T(8,128)(2,1)}), bf16[1024,1024]{1,0:T(8,128)(2,1)}) %all-gather.18.cloned.1.call-update) | async-done | bytes 2097168 | tf_op jit(solution)/shard_map/while/body/eval_jaxpr/all_gather | solution.py:179
  395.0 75.6 %reduce-scatter.27.cloned.1.call-done = f32[256,1024]{1,0:T(8,128)} async-done(((f32[1024,1024]{1,0:T(8,128)}), f32[256,1024]{1,0:T(8,128)}) %reduce-scatter.27.cloned.1.call-update) | async-done | bytes 1048592 | tf_op jit(solution)/shard_map/while/body/eval_jaxpr/reduce_scatter | solution.py:186
  481.8 48.6 %all-to-all-done = bf16[4,256,1024]{2,1,0:T(8,128)(2,1)} async-done(((bf16[4,256,1024]{2,1,0:T(8,128)(2,1)}), bf16[4,256,1024]{2,1,0:T(8,128)(2,1)}, u32[]{:S(2)}, u32[]{:S(2)}) %all-to-all-start) | async-done | bytes 2097184 | tf_op jit(solution)/shard_map/while/body/eval_jaxpr/all_to_all | solution.py:192
  594.4 21.7 %reduce-scatter.29.cloned.1.call-done = bf16[256,1024]{1,0:T(8,128)(2,1)} async-done(((bf16[1024,1024]{1,0:T(8,128)(2,1)}), bf16[256,1024]{1,0:T(8,128)(2,1)}) %reduce-scatter.29.cloned.1.call-update) | async-done | bytes 524304 | tf_op jit(solution)/shard_map/while/body/eval_jaxpr/reduce_scatter | solution.py:225
  622.7 10.2 all_gather.52
  632.9 9.5 all_gather.51
  651.6 9.5 all_gather.49
  687.7 74.8 %reduce-scatter.23.cloned.1.call-done = f32[256,1024]{1,0:T(8,128)} async-done(((f32[1024,1024]{1,0:T(8,128)}), f32[256,1024]{1,0:T(8,128)}) %reduce-scatter.23.cloned.1.call-update) | async-done | bytes 1048592 | tf_op jit(solution)/shard_map/while/body/eval_jaxpr/reduce_scatter | solution.py:152
  766.2 45.4 %all-gather.12.cloned.1.call-done = bf16[1024,1024]{1,0:T(8,128)(2,1)} async-done(((bf16[256,1024]{1,0:T(8,128)(2,1)}), bf16[1024,1024]{1,0:T(8,128)(2,1)}) %all-gather.12.cloned.1.call-update) | async-done | bytes 2097168 | tf_op jit(solution)/shard_map/while/body/eval_jaxpr/all_gather | solution.py:161
  811.5 15.0 %multiply_convert_fusion.5 = (bf16[1024,1024]{1,0:T(8,128)(2,1)}, f32[1024,1024]{1,0:T(8,128)}, f32[1024,1024]{1,0:T(8,128)}) fusion(f32[1024]{0:T(1024)S(1)} %get-tuple-element.881, bf16[1024,1024]{1,0:T(8,128)(2,1)} %all-gather.12.cloned.1.call-done, bf16[1024,1024]{1,0:T(8,128)(2,1)} %all-gather.14.cloned.1.call-done), kind=kOutput, calls=%fused_computation.26.clone.1 | convolution fusion | flops 2216689664 | bytes 14684160 | tf_op jit(solution)/shard_map/while/body/eval_jaxpr/dot_general | solution.py:162
  826.5 13.7 all-gather.16.cloned.1.call-done
  847.6 76.2 %reduce-scatter.25.cloned.1.call-done = f32[256,1024]{1,0:T(8,128)} async-done(((f32[1024,1024]{1,0:T(8,128)}), f32[256,1024]{1,0:T(8,128)}) %reduce-scatter.25.cloned.1.call-update) | async-done | bytes 1048592 | tf_op jit(solution)/shard_map/while/body/eval_jaxpr/reduce_scatter | solution.py:165
  932.3 46.2 %all-gather.18.cloned.1.call-done = bf16[1024,1024]{1,0:T(8,128)(2,1)} async-done(((bf16[256,1024]{1,0:T(8,128)(2,1)}), bf16[1024,1024]{1,0:T(8,128)(2,1)}) %all-gather.18.cloned.1.call-update) | async-done | bytes 2097168 | tf_op jit(solution)/shard_map/while/body/eval_jaxpr/all_gather | solution.py:179
  993.4 75.6 %reduce-scatter.27.cloned.1.call-done = f32[256,1024]{1,0:T(8,128)} async-done(((f32[1024,1024]{1,0:T(8,128)}), f32[256,1024]{1,0:T(8,128)}) %reduce-scatter.27.cloned.1.call-update) | async-done | bytes 1048592 | tf_op jit(solution)/shard_map/while/body/eval_jaxpr/reduce_scatter | solution.py:186
  1080.3 48.5 %all-to-all-done = bf16[4,256,1024]{2,1,0:T(8,128)(2,1)} async-done(((bf16[4,256,1024]{2,1,0:T(8,128)(2,1)}), bf16[4,256,1024]{2,1,0:T(8,128)(2,1)}, u32[]{:S(2)}, u32[]{:S(2)}) %all-to-all-start) | async-done | bytes 2097184 | tf_op jit(solution)/shard_map/while/body/eval_jaxpr/all_to_all | solution.py:192
  1197.6 17.1 %reduce-scatter.29.cloned.1.call-done = bf16[256,1024]{1,0:T(8,128)(2,1)} async-done(((bf16[1024,1024]{1,0:T(8,128)(2,1)}), bf16[256,1024]{1,0:T(8,128)(2,1)}) %reduce-scatter.29.cloned.1.call-update) | async-done | bytes 524304 | tf_op jit(solution)/shard_map/while/body/eval_jaxpr/reduce_scatter | solution.py:225
  1226.3 14.1 all-reduce.1
  1240.4 39.6 %all-reduce = (f32[1024]{0:T(1024)}, f32[1024]{0:T(1024)}, f32[1024]{0:T(1024)}, f32[1024]{0:T(1024)}, f32[1024]{0:T(1024)}, /*index=5*/f32[1024]{0:T(1024)}) all-reduce(f32[1024]{0:T(1024)S(1)} %copy-done.62, f32[1024]{0:T(1024)S(1)} %copy-done.59, f32[1024]{0:T(1024)S(1)} %copy-done.56, ...), channel_id=1, replica_groups=mesh['dp'=8,'tensor'=4] {'dp','tensor'}, use_global_device_ids=true, to_apply=%region_35.36 | all-reduce | flops 6144 | bytes 49152 | tf_op jit(solution)/shard_map/psum | solution.py:284
  1280.0 18.6 %reduce-scatter.15.cloned.1.call-done = f32[128,256]{1,0:T(8,128)} async-done(((f32[1024,256]{1,0:T(8,128)}), f32[128,256]{1,0:T(8,128)}) %reduce-scatter.15.cloned.1.call-update) | async-done | bytes 131088 | tf_op jit(solution)/shard_map/reduce_scatter | solution.py:274
  1298.6 39.6 %reduce-scatter.11.cloned.1.call-done = f32[128,256]{1,0:T(8,128)} async-done(((f32[1024,256]{1,0:T(8,128)}), f32[128,256]{1,0:T(8,128)}) %reduce-scatter.11.cloned.1.call-update) | async-done | bytes 131088 | tf_op jit(solution)/shard_map/reduce_scatter | solution.py:270
  1338.2 39.7 %reduce-scatter.13.cloned.1.call-done = f32[128,256]{1,0:T(8,128)} async-done(((f32[1024,256]{1,0:T(8,128)}), f32[128,256]{1,0:T(8,128)}) %reduce-scatter.13.cloned.1.call-update) | async-done | bytes 131088 | tf_op jit(solution)/shard_map/reduce_scatter | solution.py:271
  1378.0 55.2 %reduce-scatter.19.cloned.1.call-done = f32[128,1024]{1,0:T(8,128)} async-done(((f32[1024,1024]{1,0:T(8,128)}), f32[128,1024]{1,0:T(8,128)}) %reduce-scatter.19.cloned.1.call-update) | async-done | bytes 524304 | tf_op jit(solution)/shard_map/reduce_scatter | solution.py:277
  1433.1 55.5 %reduce-scatter.21.cloned.1.call-done = f32[1024,128]{1,0:T(8,128)} async-done(((f32[1024,1024]{1,0:T(8,128)}), f32[1024,128]{1,0:T(8,128)}) %reduce-scatter.21.cloned.1.call-update) | async-done | bytes 524304 | tf_op jit(solution)/shard_map/reduce_scatter | solution.py:281
  (548 shorter events, 323.2 us)
Async XLA Ops:
  16.6 308.8 %copy-start.27 = (f32[1024]{0:T(1024)}, f32[1024]{0:T(1024)S(1)}, u32[]{:S(2)}) copy-start(f32[1024]{0:T(1024)S(1)} %get-tuple-element.879) | copy-start | bytes 12292 | tf_op jit(solution)/shard_map/while
  16.6 308.8 %copy-start.39 = (f32[1024]{0:T(1024)}, f32[1024]{0:T(1024)S(1)}, u32[]{:S(2)}) copy-start(f32[1024]{0:T(1024)S(1)} %get-tuple-element.883) | copy-start | bytes 12292 | tf_op jit(solution)/shard_map/while
  16.6 312.9 %copy-start.23 = (f32[1024]{0:T(1024)}, f32[1024]{0:T(1024)S(1)}, u32[]{:S(2)}) copy-start(f32[1024]{0:T(1024)S(1)} %get-tuple-element.874) | copy-start | bytes 12292 | tf_op jit(solution)/shard_map/while
  16.6 363.5 %copy-start.72 = (f32[1024]{0:T(1024)}, f32[1024]{0:T(1024)S(1)}, u32[]{:S(2)}) copy-start(f32[1024]{0:T(1024)S(1)} %get-tuple-element.881) | copy-start | bytes 12292 | tf_op jit(solution)/shard_map/while
  16.6 51.7 %all-gather.10.cloned.1.call-start = ((), (), s32[]{:S(2)}) async-start(), calls=%async_computation.17 | async-start | bytes 2621440 | tf_op jit(solution)/shard_map/while/body/eval_jaxpr/all_gather | solution.py:133
  18.6 145.6 %reduce-scatter.23.cloned.1.call-start = ((), (), s32[]{:S(2)}) async-start(), calls=%async_computation.18 | async-start | bytes 5242880 | tf_op jit(solution)/shard_map/while/body/eval_jaxpr/reduce_scatter | solution.py:152
  88.5 79.4 %all-gather.14.cloned.1.call-start = ((), (), s32[]{:S(2)}) async-start(), calls=%async_computation.20 | async-start | bytes 2359296 | tf_op jit(solution)/shard_map/while/body/eval_jaxpr/all_gather | solution.py:75
  89.1 124.1 %all-gather.12.cloned.1.call-start = ((), (), s32[]{:S(2)}) async-start(), calls=%async_computation.19 | async-start | bytes 2621440 | tf_op jit(solution)/shard_map/while/body/eval_jaxpr/all_gather | solution.py:161
  167.0 74.9 %all-gather.16.cloned.1.call-start = ((), (), s32[]{:S(2)}) async-start(), calls=%async_computation.21 | async-start | bytes 2359296 | tf_op jit(solution)/shard_map/while/body/eval_jaxpr/all_gather | solution.py:79
  167.5 157.9 %reduce-scatter.25.cloned.1.call-start = ((), (), s32[]{:S(2)}) async-start(), calls=%async_computation.22 | async-start | bytes 5242880 | tf_op jit(solution)/shard_map/while/body/eval_jaxpr/reduce_scatter | solution.py:165
  248.6 131.6 %all-gather.18.cloned.1.call-start = ((), (), s32[]{:S(2)}) async-start(), calls=%async_computation.23 | async-start | bytes 2621440 | tf_op jit(solution)/shard_map/while/body/eval_jaxpr/all_gather | solution.py:179
  333.7 137.0 %reduce-scatter.27.cloned.1.call-start = ((), (), s32[]{:S(2)}) async-start(), calls=%async_computation.24 | async-start | bytes 5242880 | tf_op jit(solution)/shard_map/while/body/eval_jaxpr/reduce_scatter | solution.py:186
  477.1 53.3 %all-to-all-start = ((bf16[4,256,1024]{2,1,0:T(8,128)(2,1)}), bf16[4,256,1024]{2,1,0:T(8,128)(2,1)}, u32[]{:S(2)}, u32[]{:S(2)}) async-start(bf16[4,256,1024]{2,1,0:T(8,128)(2,1)} %stack.4), calls=%async_computation.3 | async-start | bytes 4194304 | tf_op jit(solution)/shard_map/while/body/eval_jaxpr/all_to_all | solution.py:192
  481.6 134.6 %reduce-scatter.29.cloned.1.call-start = ((), (), s32[]{:S(2)}) async-start(), calls=%async_computation.25 | async-start | bytes 2621440 | tf_op jit(solution)/shard_map/while/body/eval_jaxpr/reduce_scatter | solution.py:225
  618.8 309.1 %copy-start.23 = (f32[1024]{0:T(1024)}, f32[1024]{0:T(1024)S(1)}, u32[]{:S(2)}) copy-start(f32[1024]{0:T(1024)S(1)} %get-tuple-element.874) | copy-start | bytes 12292 | tf_op jit(solution)/shard_map/while
  618.8 359.7 %copy-start.72 = (f32[1024]{0:T(1024)}, f32[1024]{0:T(1024)S(1)}, u32[]{:S(2)}) copy-start(f32[1024]{0:T(1024)S(1)} %get-tuple-element.881) | copy-start | bytes 12292 | tf_op jit(solution)/shard_map/while
  618.8 47.8 %all-gather.10.cloned.1.call-start = ((), (), s32[]{:S(2)}) async-start(), calls=%async_computation.17 | async-start | bytes 2621440 | tf_op jit(solution)/shard_map/while/body/eval_jaxpr/all_gather | solution.py:133
  620.8 141.7 %reduce-scatter.23.cloned.1.call-start = ((), (), s32[]{:S(2)}) async-start(), calls=%async_computation.18 | async-start | bytes 5242880 | tf_op jit(solution)/shard_map/while/body/eval_jaxpr/reduce_scatter | solution.py:152
  686.9 79.3 %all-gather.14.cloned.1.call-start = ((), (), s32[]{:S(2)}) async-start(), calls=%async_computation.20 | async-start | bytes 2359296 | tf_op jit(solution)/shard_map/while/body/eval_jaxpr/all_gather | solution.py:75
  687.6 123.9 %all-gather.12.cloned.1.call-start = ((), (), s32[]{:S(2)}) async-start(), calls=%async_computation.19 | async-start | bytes 2621440 | tf_op jit(solution)/shard_map/while/body/eval_jaxpr/all_gather | solution.py:161
  765.3 75.0 %all-gather.16.cloned.1.call-start = ((), (), s32[]{:S(2)}) async-start(), calls=%async_computation.21 | async-start | bytes 2359296 | tf_op jit(solution)/shard_map/while/body/eval_jaxpr/all_gather | solution.py:79
  765.9 157.9 %reduce-scatter.25.cloned.1.call-start = ((), (), s32[]{:S(2)}) async-start(), calls=%async_computation.22 | async-start | bytes 5242880 | tf_op jit(solution)/shard_map/while/body/eval_jaxpr/reduce_scatter | solution.py:165
  846.9 131.6 %all-gather.18.cloned.1.call-start = ((), (), s32[]{:S(2)}) async-start(), calls=%async_computation.23 | async-start | bytes 2621440 | tf_op jit(solution)/shard_map/while/body/eval_jaxpr/all_gather | solution.py:179
  932.0 137.0 %reduce-scatter.27.cloned.1.call-start = ((), (), s32[]{:S(2)}) async-start(), calls=%async_computation.24 | async-start | bytes 5242880 | tf_op jit(solution)/shard_map/while/body/eval_jaxpr/reduce_scatter | solution.py:186
  1075.4 53.3 %all-to-all-start = ((bf16[4,256,1024]{2,1,0:T(8,128)(2,1)}), bf16[4,256,1024]{2,1,0:T(8,128)(2,1)}, u32[]{:S(2)}, u32[]{:S(2)}) async-start(bf16[4,256,1024]{2,1,0:T(8,128)(2,1)} %stack.4), calls=%async_computation.3 | async-start | bytes 4194304 | tf_op jit(solution)/shard_map/while/body/eval_jaxpr/all_to_all | solution.py:192
  1079.9 134.8 %reduce-scatter.29.cloned.1.call-start = ((), (), s32[]{:S(2)}) async-start(), calls=%async_computation.25 | async-start | bytes 2621440 | tf_op jit(solution)/shard_map/while/body/eval_jaxpr/reduce_scatter | solution.py:225
  1219.1 60.9 %reduce-scatter.17.cloned.1.call-start = ((), (), s32[]{:S(2)}) async-start(), calls=%async_computation.14 | async-start | bytes 1179648 | tf_op jit(solution)/shard_map/reduce_scatter | solution.py:280
  1219.7 78.9 %reduce-scatter.15.cloned.1.call-start = ((), (), s32[]{:S(2)}) async-start(), calls=%async_computation.13 | async-start | bytes 1179648 | tf_op jit(solution)/shard_map/reduce_scatter | solution.py:274
  1223.5 114.7 %reduce-scatter.11.cloned.1.call-start = ((), (), s32[]{:S(2)}) async-start(), calls=%async_computation.11 | async-start | bytes 1179648 | tf_op jit(solution)/shard_map/reduce_scatter | solution.py:270
  1224.1 153.9 %reduce-scatter.13.cloned.1.call-start = ((), (), s32[]{:S(2)}) async-start(), calls=%async_computation.12 | async-start | bytes 1179648 | tf_op jit(solution)/shard_map/reduce_scatter | solution.py:271
  1224.8 208.3 %reduce-scatter.19.cloned.1.call-start = ((), (), s32[]{:S(2)}) async-start(), calls=%async_computation.15 | async-start | bytes 4718592 | tf_op jit(solution)/shard_map/reduce_scatter | solution.py:277
  1225.6 263.1 %reduce-scatter.21.cloned.1.call-start = ((), (), s32[]{:S(2)}) async-start(), calls=%async_computation.16 | async-start | bytes 4718592 | tf_op jit(solution)/shard_map/reduce_scatter | solution.py:281
  (155 other events, 2340.7 us)
Sparse Core Ops, SparseCore 0:
  19.6 48.6 all-gather.9
  88.6 75.4 reduce-scatter.22
  333.8 46.3 all-gather.17
  395.1 75.4 reduce-scatter.26
  621.5 45.1 all-gather.9
  687.0 75.4 reduce-scatter.22
  932.1 46.3 all-gather.17
  993.5 75.4 reduce-scatter.26
Sparse Core Ops, SparseCore 1:
  91.0 26.4 all-gather.13
  167.0 46.0 all-gather.11
  215.0 26.8 all-gather.15
  248.7 76.7 reduce-scatter.24
  573.9 42.2 reduce-scatter.28
  689.7 26.4 all-gather.13
  765.4 46.1 all-gather.11
  813.4 26.8 all-gather.15
  847.0 76.7 reduce-scatter.24
  1172.5 42.2 reduce-scatter.28
  1223.3 35.5 reduce-scatter.16
  1262.7 35.9 reduce-scatter.14
  1302.2 35.9 reduce-scatter.10
  1342.0 35.9 reduce-scatter.12
  1381.9 51.2 reduce-scatter.18
  1437.5 51.1 reduce-scatter.20
